TPU v7x, 32 devices: a whole 2x2x4 slice. The times are simulated.
32 devices in a mesh: outer: 4 (over y, x), inner: 8 (over z, core).
Axes of the slice: x: 2, y: 2, z: 4, core: 2. Of those that a mesh axis runs over, the one named last changes fastest.
Arguments:
- queries: bfloat16 [8192, 1024], P(('outer', 'inner')), may hold values from -6 to 6
- keys: bfloat16 [2, 8192, 1024], P(None, ('outer', 'inner')), may hold values from -6 to 6
- values: bfloat16 [2, 8192, 1024], P(None, ('outer', 'inner')), may hold values from -6 to 6
- betas: float32 [2, 8, 8192], P(None, None, ('outer', 'inner')), may hold values from 0 to 2
- log_decay: float32 [8, 8192], P(None, ('outer', 'inner')), may hold values from -1 to 0
- out_gain: float32 [128], replicated, may hold values from 0.5 to 1.5
Outputs:
- mixed: bfloat16 [8192, 1024], P(('outer', 'inner'))
All inputs are finite; a program needn't handle non-finite values.
Results may differ from a plain program's by a relative error of at most 0.0018.
Values sent between devices are 32-bit elements; how exact they have to be, the bound alone decides.
A program may use at most 128 MiB of HBM per device.

v0:
```python
import jax
import jax.numpy as jnp
from jax import lax
from jax.sharding import PartitionSpec as P

BLOCK_LEN = 64
HIGHEST = lax.Precision.HIGHEST


def entering(part, axis, combine, identity):
    place = lax.axis_index(axis)
    gathered = jax.tree.map(lambda a: lax.all_gather(a, axis), part)
    state = jax.tree.map(lambda a, e: jnp.zeros_like(a) + jnp.asarray(e, a.dtype), part, identity)

    def one(hop, state):
        return combine(
            state, jax.tree.map(lambda a: lax.dynamic_index_in_dim(a, hop, 0, False), gathered)
        )

    return lax.fori_loop(0, place, one, state)


def spread(x, axis, root):
    mine = lax.axis_index(axis) == root
    return lax.psum(jnp.where(mine, x, jnp.zeros_like(x)), axis)


def prepare(queries, keys, values, betas, log_decay, span):
    length = queries.shape[0]
    heads = betas.shape[1]
    width_k = queries.shape[1] // heads
    width_v = values.shape[2] // heads
    blocks = length // span
    reflect = 2 * span
    query_b = queries.reshape(blocks, span, heads, width_k).transpose(0, 2, 1, 3)
    query_f = query_b.astype(jnp.float32)
    query_inv = lax.rsqrt(jnp.sum(query_f * query_f, -1) + 1e-06)
    query_n = query_f * query_inv[..., None]
    key_b = (
        keys.reshape(2, blocks, span, heads, width_k)
        .transpose(1, 3, 2, 0, 4)
        .reshape(blocks, heads, reflect, width_k)
    )
    key_f = key_b.astype(jnp.float32)
    key_inv = lax.rsqrt(jnp.sum(key_f * key_f, -1) + 1e-06)
    key_n = key_f * key_inv[..., None]
    value_n = (
        values.astype(jnp.float32).reshape(2, blocks, span, heads, width_v).transpose(1, 3, 2, 0, 4)
    )
    value_n = value_n.reshape(blocks, heads, reflect, width_v)
    beta_r = (
        betas.reshape(2, heads, blocks, span).transpose(2, 1, 3, 0).reshape(blocks, heads, reflect)
    )
    decay_t = log_decay.reshape(heads, blocks, span).transpose(1, 0, 2)
    decay_r = jnp.stack([decay_t, jnp.zeros_like(decay_t)], -1).reshape(blocks, heads, reflect)
    cumulative = jnp.cumsum(decay_r, -1)
    row_idx = lax.broadcasted_iota(jnp.int32, (reflect, reflect), 0)
    col_idx = lax.broadcasted_iota(jnp.int32, (reflect, reflect), 1)
    key_gram = (
        jnp.einsum("nhrd,nhsd->nhrs", key_b, key_b, preferred_element_type=jnp.float32)
        * key_inv[..., :, None]
        * key_inv[..., None, :]
    )
    fall_off = jnp.exp(jnp.minimum(cumulative[..., :, None] - cumulative[..., None, :], 0.0))
    strict_low = jnp.where(row_idx > col_idx, key_gram * fall_off, 0.0)
    system = jnp.eye(reflect, dtype=jnp.float32) + beta_r[..., :, None] * strict_low
    scaled = jnp.exp(cumulative)
    right_side = jnp.concatenate(
        [(beta_r * scaled)[..., None] * key_n, beta_r[..., None] * value_n], -1
    )
    solved = lax.linalg.triangular_solve(
        system, right_side, left_side=True, lower=True, unit_diagonal=True
    )
    write_key = solved[..., :width_k]
    write_val = solved[..., width_k:]
    tok_idx = lax.broadcasted_iota(jnp.int32, (span, reflect), 0)
    ref_idx = lax.broadcasted_iota(jnp.int32, (span, reflect), 1)
    query_cum = cumulative.reshape(blocks, heads, span, 2)[..., 1]
    query_key = (
        jnp.einsum("nhcd,nhsd->nhcs", query_b, key_b, preferred_element_type=jnp.float32)
        * query_inv[..., :, None]
        * key_inv[..., None, :]
    )
    fade = jnp.exp(jnp.minimum(query_cum[..., :, None] - cumulative[..., None, :], 0.0))
    reach = jnp.where(ref_idx <= 2 * tok_idx + 1, query_key * fade, 0.0)
    reduced = jnp.exp(query_cum)[..., None] * query_n - jnp.einsum(
        "nhcs,nhsd->nhcd", reach, write_key, precision=HIGHEST
    )
    local_out = jnp.einsum("nhcs,nhsd->nhcd", reach, write_val, precision=HIGHEST)
    last_cum = cumulative[..., -1:]
    tail = jnp.exp(last_cum - cumulative)
    trans = jnp.exp(last_cum)[..., None] * jnp.eye(width_k, dtype=jnp.float32)
    trans = trans - jnp.einsum(
        "nhsd,nhse->nhde", tail[..., None] * write_key, key_n, precision=HIGHEST
    )
    inject = jnp.einsum("nhsd,nhse->nhde", tail[..., None] * write_val, key_n, precision=HIGHEST)
    return (reduced, local_out, trans, inject)


def compose(earlier, later):
    new_map = jnp.einsum("hde,hef->hdf", earlier[0], later[0], precision=HIGHEST)
    new_add = jnp.einsum("hde,hef->hdf", earlier[1], later[0], precision=HIGHEST) + later[1]
    return (new_map, new_add)


def advance(state_pair, inputs):
    prefix_map, prefix_add = state_pair
    red_b, loc_b, trans_b, inj_b = inputs
    carried = jnp.einsum("hcd,hed->hce", red_b, prefix_map, precision=HIGHEST)
    base_out = jnp.einsum("hcd,hed->hce", red_b, prefix_add, precision=HIGHEST) + loc_b
    next_pair = compose((prefix_map, prefix_add), (trans_b, inj_b))
    return (next_pair, (carried, base_out))


def per_device(queries, keys, values, betas, log_decay, out_gain):
    heads = betas.shape[1]
    width_k = queries.shape[1] // heads
    width_v = values.shape[2] // heads
    reduced, local_out, trans, inject = prepare(queries, keys, values, betas, log_decay, BLOCK_LEN)
    identity = (
        jnp.broadcast_to(jnp.eye(width_k, dtype=jnp.float32), (heads, width_k, width_k)),
        jnp.zeros((heads, width_v, width_k), jnp.float32),
    )
    own_pair, pieces = lax.scan(advance, identity, (reduced, local_out, trans, inject))
    carried, base_out = pieces
    before_map, before_add = entering(own_pair, "inner", compose, identity)
    through = compose((before_map, before_add), own_pair)
    group_map, group_add = (
        spread(through[0], "inner", lax.axis_size("inner") - 1),
        spread(through[1], "inner", lax.axis_size("inner") - 1),
    )
    group_state = entering((group_map, group_add), "outer", compose, identity)[1]
    entering_state = (
        jnp.einsum("hde,hef->hdf", group_state, before_map, precision=HIGHEST) + before_add
    )
    readout = jnp.einsum("nhcd,hed->nhce", carried, entering_state, precision=HIGHEST) + base_out
    mean_sq = jnp.mean(readout * readout, -1, keepdims=True)
    normed = readout * lax.rsqrt(mean_sq + 1e-05) * out_gain
    blocks = normed.shape[0]
    return (
        normed.transpose(0, 2, 1, 3)
        .reshape(blocks * BLOCK_LEN, heads * width_v)
        .astype(jnp.bfloat16)
    )


def solution(mesh):
    placed = (
        P(("outer", "inner"), None),
        P(None, ("outer", "inner"), None),
        P(None, ("outer", "inner"), None),
        P(None, None, ("outer", "inner")),
        P(None, ("outer", "inner")),
        P(),
    )
    return jax.shard_map(
        per_device,
        mesh=mesh,
        in_specs=placed,
        out_specs=P(("outer", "inner"), None),
        check_vma=False,
    )
```

profile of v0, /device:TPU:6, one launch (start us, length us, event | category | flops | bytes accessed | tf_op | source)
XLA Modules:
  0.0 689.7 jit_solution(12705137376245005066)
XLA Ops:
  6.5 1.5 copy.206
  8.0 2.3 multiply_reduce_fusion
  10.3 1.1 copy.136
  11.8 1.1 reduce_window_sum.11
  14.4 3.4 add_bitcast_fusion
  17.8 315.9 %custom-call.3 = f32[4,8,1,128,128]{3,4,2,1,0:T(8,128)} custom-call(f32[4,8,1,128,128]{4,3,2,1,0:T(8,128)} %add_bitcast_fusion), custom_call_target="InvertDiagBlocksLowerTriangular" | custom-call | tf_op jit(solution)/shard_map/triangular_solve | solution.py:71
  333.8 2.2 fusion.44
  336.3 1.6 copy.142
  337.9 1.9 broadcast_multiply_fusion
  340.8 6.6 fusion.35
  348.3 3.0 fusion.45
  351.2 3.0 fusion.53
  354.3 6.0 fusion.40
  360.3 6.2 multiply_subtract_fusion
  366.6 31.3 %while.43 = (s32[]{:T(128)}, f32[8,128,128]{1,2,0:T(8,128)S(1)}, f32[8,128,128]{1,2,0:T(8,128)S(1)}, f32[4,8,64,128]{3,2,0,1:T(8,128)}, f32[4,8,64,128]{3,2,0,1:...) while((s32[]{:T(128)}, f32[8,128,128]{1,2,0:T(8,128)S(1)}, ...), condition=%wide.region_4.5_spmd.clone, body=%wide.region_3.4_spmd.clone.sunk | while | flops 604438528 | bytes 8129660 | solution.py:124
  366.6 2.3 fusion.131
  369.0 2.1 fusion.129
  371.1 2.3 fusion.130
  373.4 1.0 convolution_bitcast_fusion.10
  374.5 2.3 fusion.131
  376.8 2.1 fusion.129
  378.9 2.3 fusion.130
  381.2 1.0 convolution_bitcast_fusion.10
  382.3 2.3 fusion.131
  384.6 2.1 fusion.129
  386.7 2.3 fusion.130
  389.0 1.0 convolution_bitcast_fusion.10
  390.1 2.3 fusion.131
  392.4 2.1 fusion.129
  394.5 2.3 fusion.130
  396.8 1.0 convolution_bitcast_fusion.10
  400.0 47.1 %all-gather.11.cloned.1.call-done = f32[64,128,128]{2,1,0:T(8,128)} async-done(((f32[8,128,128]{2,1,0:T(8,128)}), f32[64,128,128]{2,1,0:T(8,128)}) %all-gather.11.cloned.1.call-update) | async-done | bytes 4194320 | tf_op jit(solution)/shard_map/all_gather | solution.py:12
  447.1 47.3 %all-gather.13.cloned.1.call-done = f32[64,128,128]{2,1,0:T(8,128)} async-done(((f32[8,128,128]{2,1,0:T(8,128)}), f32[64,128,128]{2,1,0:T(8,128)}) %all-gather.13.cloned.1.call-update) | async-done | bytes 4194320 | tf_op jit(solution)/shard_map/all_gather | solution.py:12
  494.5 1.0 copy-done.1
  495.5 1.9 fusion.63
  497.4 1.8 fusion.60
  499.3 96.0 %all-reduce.4.cloned.1.call-done = (f32[1,8,128,128]{3,2,1,0:T(8,128)}, f32[1,8,128,128]{3,2,1,0:T(8,128)}) async-done(((f32[1,8,128,128]{3,2,1,0:T(8,128)}, f32[1,8,128,128]{3,2,1,0:T(8,128)}), (f32[1,8,128,128]{3,2,1,0:T(8,128)}, f32[1,8,128,128]{3,2,1,0:T(8,128)})) %all-reduce.4.cloned.1.call-update) | async-done | bytes 1048592 | tf_op jit(solution)/shard_map/psum | solution.py:25
  596.0 34.3 %all-gather.7.cloned.1.call-done = f32[4,8,128,128]{3,2,1,0:T(8,128)} async-done(((f32[1,8,128,128]{3,2,1,0:T(8,128)}), f32[4,8,128,128]{3,2,1,0:T(8,128)}) %all-gather.7.cloned.1.call-update) | async-done | bytes 2097168 | tf_op jit(solution)/shard_map/all_gather | solution.py:12
  630.4 36.9 %all-gather.9.cloned.1.call-done = f32[4,8,128,128]{3,2,1,0:T(8,128)} async-done(((f32[1,8,128,128]{3,2,1,0:T(8,128)}), f32[4,8,128,128]{3,2,1,0:T(8,128)}) %all-gather.9.cloned.1.call-update) | async-done | bytes 2097168 | tf_op jit(solution)/shard_map/all_gather | solution.py:12
  667.3 10.5 %while.42 = (s32[]{:T(128)}, f32[8,128,128]{1,2,0:T(8,128)S(1)}, s32[]{:T(128)}, f32[4,8,128,128]{3,2,1,0:T(8,128)}, f32[4,8,128,128]{3,2,1,0:T(8,128)}, /*index=5*/s32[]{:T(128)}, s32[]{:T(128)}, s32[]{:T(128)}) while((s32[]{:T(128)}, f32[8,128,128]{1,2,0:T(8,128)S(1)}, s32[]{:T(128)}, f32[4,8,128,128]{3,2,1,0:T(8,128)}, ...), condition=%wide.region_10.11_spmd, body=%wide.region_9.10_spmd.sunk | while | flops 201457664 | bytes 5243007 | solution.py:20
  667.3 1.1 constant_dynamic-slice_fusion.5
  668.7 2.1 fusion.120
  670.8 1.1 constant_dynamic-slice_fusion.5
  672.1 2.1 fusion.120
  674.2 1.1 constant_dynamic-slice_fusion.5
  675.5 2.1 fusion.120
  677.9 1.0 fusion.61
  679.1 2.5 multiply_reduce_fusion.1
  (80 shorter events, 9.7 us)
Async XLA Ops:
  6.5 440.6 %all-gather.11.cloned.1.call-start = ((), (), s32[]{:S(2)}) async-start(), calls=%async_computation.2 | async-start | bytes 4718592 | tf_op jit(solution)/shard_map/all_gather | solution.py:12
  8.0 3.4 copy-start.6
  10.3 3.6 copy-start.5
  11.4 342.8 %copy-start = (bf16[2,4,64,8,128]{4,0,2,3,1:T(2,128)(2,1)}, bf16[2,4,64,8,128]{4,0,2,3,1:T(2,128)(2,1)S(1)}, u32[]{:S(2)}) copy-start(bf16[2,4,64,8,128]{4,0,2,3,1:T(2,128)(2,1)S(1)} %copy.136) | copy-start | bytes 3145732
  17.8 318.2 %copy-start.2 = (bf16[2,256,1024]{2,1,0:T(8,128)(2,1)S(1)}, bf16[2,256,1024]{2,1,0:T(8,128)(2,1)}, u32[]{:S(2)}) copy-start(bf16[2,256,1024]{2,1,0:T(8,128)(2,1)} %param.14) | copy-start | bytes 3145732
  337.9 2.2 copy-start.4
  398.9 95.5 %all-gather.13.cloned.1.call-start = ((), (), s32[]{:S(2)}) async-start(), calls=%async_computation.3 | async-start | bytes 4718592 | tf_op jit(solution)/shard_map/all_gather | solution.py:12
  400.0 195.2 %all-reduce.4.cloned.1.call-start = ((), (), s32[]{:S(2)}) async-start(), calls=%async_computation.4 | async-start | bytes 2097152 | tf_op jit(solution)/shard_map/psum | solution.py:25
  494.5 1.0 copy-start.1
  499.2 131.1 %all-gather.7.cloned.1.call-start = ((), (), s32[]{:S(2)}) async-start(), calls=%async_computation | async-start | bytes 2621440 | tf_op jit(solution)/shard_map/all_gather | solution.py:12
  595.3 72.0 %all-gather.9.cloned.1.call-start = ((), (), s32[]{:S(2)}) async-start(), calls=%async_computation.1 | async-start | bytes 2621440 | tf_op jit(solution)/shard_map/all_gather | solution.py:12
  677.9 1.2 copy-start.3
  678.9 2.7 copy-start.7
Sparse Core Ops, SparseCore 0:
  399.0 48.0 all-gather.10
  448.7 45.6 all-gather.12
  499.3 95.8 all-reduce.3
  596.9 33.3 all-gather.6
  632.1 35.1 all-gather.8
where the time goes:
time: 692 us; the launch traced here: 690 us
  other arithmetic  324 us (47%)
  waiting for transfers between devices  262 us (38%)
  matrix products  73.3 us (11%)
  local copies, waits for them, and re-layouts  15.5 us (2%)
  between operations  13.5 us (2%)
    another operation x2, other arithmetic, prepare(): lax.linalg.triangular_solve(system, right_side, left_side=True, lower=Tru...  316 us
    all_gather x4, waiting for transfers between devices, entering(): gathered = jax.tree.map(lambda a: lax.all_gather(a, axis), part)  166 us
    psum x1, waiting for transfers between devices, spread(): return lax.psum(jnp.where(mine, x, jnp.zeros_like(x)), axis)  96 us
    dot_general x8, matrix products, compose(): jnp.einsum('hde,hef->hdf', earlier[1], later[0], precision=HIGHEST)  16.2 us
  transfers between devices with their start and end apart: 5, of which 5 were waited for; matrix products, arithmetic and copies ran while one was open for 0% of the time, Pallas kernels for 0%

commit v1 on v0

--- a/solution.py
+++ b/solution.py
@@ -5,6 +5,12 @@
 
 BLOCK_LEN = 64
 HIGHEST = lax.Precision.HIGHEST
+
+
+def summed_here(x, mesh_axis):
+    shards = lax.all_gather(x, mesh_axis, axis=0, tiled=False)
+    total = shards.sum(axis=0)
+    return total
 
 
 def entering(part, axis, combine, identity):
@@ -22,7 +28,7 @@
 
 def spread(x, axis, root):
     mine = lax.axis_index(axis) == root
-    return lax.psum(jnp.where(mine, x, jnp.zeros_like(x)), axis)
+    return summed_here(jnp.where(mine, x, jnp.zeros_like(x)), axis)
 
 
 def prepare(queries, keys, values, betas, log_decay, span):

time: 692 us -> 740 us (1.069)
  waiting for transfers between devices: 262 us -> 288 us
  matrix products: 73.3 us -> 82.6 us
    all_gather x0 -> x2, waiting for transfers between devices: none -> 125 us  [summed_here(): shards = lax.all_gather(x, mesh_axis, axis=0, tiled=False)]
    psum x1 -> x0, waiting for transfers between devices: 96 us -> none  [spread(): return lax.psum(jnp.where(mine, x, jnp.zeros_like(x)), axis)]
    dot_general x1, matrix products: 6.01 us -> 15.3 us  [prepare(): jnp.einsum('nhsd,nhse->nhde', tail[..., None] * write_val, key_n, precisi...]
  transfers between devices with their start and end apart: 5 -> 6, of which waited for: 5 -> 6; matrix products, arithmetic and copies ran while one was open for 0% -> 1% of each run, Pallas kernels for 0% -> 0%
where the time goes in v1:
time: 740 us; the launch traced here: 732 us
  other arithmetic  331 us (45%)
  waiting for transfers between devices  288 us (39%)
  matrix products  82.6 us (11%)
  local copies, waits for them, and re-layouts  15.5 us (2%)
  between operations  14.1 us (2%)
    another operation x2, other arithmetic, prepare(): lax.linalg.triangular_solve(system, right_side, left_side=True, lower=Tru...  316 us
    all_gather x4, waiting for transfers between devices, entering(): gathered = jax.tree.map(lambda a: lax.all_gather(a, axis), part)  163 us
    all_gather x2, waiting for transfers between devices, summed_here(): shards = lax.all_gather(x, mesh_axis, axis=0, tiled=False)  125 us
    dot_general x8, matrix products, compose(): jnp.einsum('hde,hef->hdf', earlier[1], later[0], precision=HIGHEST)  16.2 us
    dot_general x1, matrix products, prepare(): jnp.einsum('nhsd,nhse->nhde', tail[..., None] * write_val, key_n, precisi...  15.3 us
  transfers between devices with their start and end apart: 6, of which 6 were waited for; matrix products, arithmetic and copies ran while one was open for 1% of the time, Pallas kernels for 0%

profile of v1, /device:TPU:6, one launch (start us, length us, event | category | flops | bytes accessed | tf_op | source)
XLA Modules:
  0.0 732.4 jit_solution(3634140454091514065)
XLA Ops:
  6.5 1.5 copy.204
  8.0 2.3 multiply_reduce_fusion
  10.3 1.1 copy.132
  11.8 1.1 reduce_window_sum.11
  14.4 3.4 add_bitcast_fusion
  17.8 315.9 %custom-call.3 = f32[4,8,1,128,128]{3,4,2,1,0:T(8,128)} custom-call(f32[4,8,1,128,128]{4,3,2,1,0:T(8,128)} %add_bitcast_fusion), custom_call_target="InvertDiagBlocksLowerTriangular" | custom-call | tf_op jit(solution)/shard_map/triangular_solve | solution.py:77
  333.8 2.6 fusion.44
  336.7 1.6 copy.138
  338.3 1.9 broadcast_multiply_fusion
  341.2 6.6 fusion.35
  348.6 3.0 fusion.45
  351.6 3.1 fusion.53
  354.7 15.3 %fusion.40 = f32[4,8,128,128]{2,3,1,0:T(8,128)} fusion(bf16[4,8,128,128]{3,2,1,0:T(8,128)(2,1)S(1)} %bitcast.191, f32[4,8,128,256]{3,2,1,0:T(8,128)S(1)} %fusion.35, f32[4,8,128]{2,1,0:T(8,128)S(1)} %copy.135, f32[4,8,128]{2,1,0:T(8,128)S(1)} %get-tuple-element.294), kind=kOutput, calls=%fused_computation.49 | convolution fusion | flops 806879232 | bytes 5275648 | tf_op jit(solution)/shard_map/nhsd,nhse->nhde/dot_general | solution.py:102
  370.0 6.2 multiply_subtract_fusion
  376.3 31.3 %while.43 = (s32[]{:T(128)}, f32[8,128,128]{1,2,0:T(8,128)S(1)}, f32[8,128,128]{1,2,0:T(8,128)S(1)}, f32[4,8,64,128]{3,2,0,1:T(8,128)}, f32[4,8,64,128]{3,2,0,1:...) while((s32[]{:T(128)}, f32[8,128,128]{1,2,0:T(8,128)S(1)}, ...), condition=%wide.region_4.5_spmd.clone, body=%wide.region_3.4_spmd.clone.sunk | while | flops 604438528 | bytes 8129660 | solution.py:130
  376.3 2.3 fusion.129
  378.6 2.1 fusion.127
  380.7 2.3 fusion.128
  383.0 1.0 convolution_bitcast_fusion.10
  384.2 2.3 fusion.129
  386.5 2.1 fusion.127
  388.6 2.3 fusion.128
  390.9 1.0 convolution_bitcast_fusion.10
  392.0 2.3 fusion.129
  394.3 2.1 fusion.127
  396.4 2.3 fusion.128
  398.7 1.0 convolution_bitcast_fusion.10
  399.8 2.3 fusion.129
  402.1 2.1 fusion.127
  404.2 2.3 fusion.128
  409.7 47.1 %all-gather.13.cloned.1.call-done = f32[64,128,128]{2,1,0:T(8,128)} async-done(((f32[8,128,128]{2,1,0:T(8,128)}), f32[64,128,128]{2,1,0:T(8,128)}) %all-gather.13.cloned.1.call-update) | async-done | bytes 4194320 | tf_op jit(solution)/shard_map/all_gather | solution.py:18
  456.8 47.3 %all-gather.15.cloned.1.call-done = f32[64,128,128]{2,1,0:T(8,128)} async-done(((f32[8,128,128]{2,1,0:T(8,128)}), f32[64,128,128]{2,1,0:T(8,128)}) %all-gather.15.cloned.1.call-update) | async-done | bytes 4194320 | tf_op jit(solution)/shard_map/all_gather | solution.py:18
  505.2 1.8 fusion.61
  507.1 1.8 convolution_select_fusion
  509.0 81.6 %all-gather.21.cloned.1.call-done = f32[64,128,128]{2,1,0:T(8,128)} async-done(((f32[8,128,128]{2,1,0:T(8,128)}), f32[64,128,128]{2,1,0:T(8,128)}) %all-gather.21.cloned.1.call-update) | async-done | bytes 4194320 | tf_op jit(solution)/shard_map/all_gather | solution.py:11
  590.6 3.3 reduce_sum.48
  594.0 43.8 %all-gather.17.cloned.1.call-done = f32[64,128,128]{2,1,0:T(8,128)} async-done(((f32[8,128,128]{2,1,0:T(8,128)}), f32[64,128,128]{2,1,0:T(8,128)}) %all-gather.17.cloned.1.call-update) | async-done | bytes 4194320 | tf_op jit(solution)/shard_map/all_gather | solution.py:11
  637.8 3.3 reduce_sum.47
  641.3 31.3 %all-gather.23.cloned.1.call-done = f32[32,128,128]{2,1,0:T(8,128)} async-done(((f32[8,128,128]{2,1,0:T(8,128)}), f32[32,128,128]{2,1,0:T(8,128)}) %all-gather.23.cloned.1.call-update) | async-done | bytes 2097168 | tf_op jit(solution)/shard_map/all_gather | solution.py:18
  672.6 36.9 %all-gather.19.cloned.1.call-done = f32[32,128,128]{2,1,0:T(8,128)} async-done(((f32[8,128,128]{2,1,0:T(8,128)}), f32[32,128,128]{2,1,0:T(8,128)}) %all-gather.19.cloned.1.call-update) | async-done | bytes 2097168 | tf_op jit(solution)/shard_map/all_gather | solution.py:18
  709.5 10.5 %while.42 = (s32[]{:T(128)}, f32[8,128,128]{1,2,0:T(8,128)S(1)}, s32[]{:T(128)}, f32[4,8,128,128]{3,2,1,0:T(8,128)}, f32[4,8,128,128]{3,2,1,0:T(8,128)}, /*index=5*/s32[]{:T(128)}, s32[]{:T(128)}, s32[]{:T(128)}) while((s32[]{:T(128)}, f32[8,128,128]{1,2,0:T(8,128)S(1)}, s32[]{:T(128)}, f32[4,8,128,128]{3,2,1,0:T(8,128)}, ...), condition=%wide.region_10.11_spmd, body=%wide.region_9.10_spmd.sunk | while | flops 201457664 | bytes 5243007 | solution.py:26
  709.5 1.1 constant_dynamic-slice_fusion.5
  710.9 2.1 fusion.118
  713.0 1.1 constant_dynamic-slice_fusion.5
  714.3 2.1 fusion.118
  716.4 1.1 constant_dynamic-slice_fusion.5
  717.7 2.1 fusion.118
  721.2 2.5 multiply_reduce_fusion.1
  (85 shorter events, 12.3 us)
Async XLA Ops:
  6.5 450.3 %all-gather.13.cloned.1.call-start = ((), (), s32[]{:S(2)}) async-start(), calls=%async_computation | async-start | bytes 4718592 | tf_op jit(solution)/shard_map/all_gather | solution.py:18
  8.0 3.4 copy-start.6
  10.3 3.6 copy-start.5
  11.4 343.3 %copy-start = (bf16[2,4,64,8,128]{4,0,2,3,1:T(2,128)(2,1)}, bf16[2,4,64,8,128]{4,0,2,3,1:T(2,128)(2,1)S(1)}, u32[]{:S(2)}) copy-start(bf16[2,4,64,8,128]{4,0,2,3,1:T(2,128)(2,1)S(1)} %copy.132) | copy-start | bytes 3145732
  17.8 318.6 %copy-start.2 = (bf16[2,256,1024]{2,1,0:T(8,128)(2,1)S(1)}, bf16[2,256,1024]{2,1,0:T(8,128)(2,1)}, u32[]{:S(2)}) copy-start(bf16[2,256,1024]{2,1,0:T(8,128)(2,1)} %param.14) | copy-start | bytes 3145732
  338.3 2.2 copy-start.4
  408.6 95.5 %all-gather.15.cloned.1.call-start = ((), (), s32[]{:S(2)}) async-start(), calls=%async_computation.1 | async-start | bytes 4718592 | tf_op jit(solution)/shard_map/all_gather | solution.py:18
  409.7 180.9 %all-gather.21.cloned.1.call-start = ((), (), s32[]{:S(2)}) async-start(), calls=%async_computation.4 | async-start | bytes 4718592 | tf_op jit(solution)/shard_map/all_gather | solution.py:11
  504.2 1.0 copy-start.1
  507.1 130.7 %all-gather.17.cloned.1.call-start = ((), (), s32[]{:S(2)}) async-start(), calls=%async_computation.2 | async-start | bytes 4718592 | tf_op jit(solution)/shard_map/all_gather | solution.py:11
  508.9 163.6 %all-gather.23.cloned.1.call-start = ((), (), s32[]{:S(2)}) async-start(), calls=%async_computation.5 | async-start | bytes 2621440 | tf_op jit(solution)/shard_map/all_gather | solution.py:18
  593.9 115.5 %all-gather.19.cloned.1.call-start = ((), (), s32[]{:S(2)}) async-start(), calls=%async_computation.3 | async-start | bytes 2621440 | tf_op jit(solution)/shard_map/all_gather | solution.py:18
  720.0 1.2 copy-start.3
  721.0 2.7 copy-start.7
Sparse Core Ops, SparseCore 0:
  408.7 48.0 all-gather.12
  458.4 45.6 all-gather.14
  507.2 83.3 all-gather.20
  592.1 45.6 all-gather.16
  639.5 33.0 all-gather.22
  674.3 35.1 all-gather.18
